TPU v7x, 256 devices: a whole 4x4x8 slice. The times are simulated.
256 devices in a mesh: ctx: 16 (over y, x), exp: 8 (over z), dp: 2 (over core).
Axes of the slice: x: 4, y: 4, z: 8, core: 2. Of those that a mesh axis runs over, the one named last changes fastest.
Arguments:
- residual: bfloat16 [2048, 4096], P('ctx', ('exp', 'dp')), may hold values from -6 to 6
- ssm_values: bfloat16 [2048, 4096], P('ctx', ('exp', 'dp')), may hold values from -6 to 6
- ssm_keys: bfloat16 [2048, 64], P('ctx'), may hold values from -6 to 6
- ssm_queries: bfloat16 [2048, 64], P('ctx'), may hold values from -0.015625 to 0.015625
- log_decay: float32 [2048, 64], P('ctx', ('exp', 'dp')), may hold values from -1 to 0, as said below
- expert_ids: int32 [2048, 2], P('ctx'), may hold values from 0 to 7, all different within a row; in each aligned block of 128 rows (0 to 127, 128 to 255, ...) at most 40 rows name the same one
- gate_probs: float32 [2048, 2], P('ctx'), may hold values from 0.2 to 1
- norm_gain: float32 [4096], P(('exp', 'dp')), may hold values from 0.5 to 1.5
- w_gate: bfloat16 [8, 4096, 8192], P('exp', None, ('ctx', 'dp')), may hold values from -0.09375 to 0.09375
- w_up: bfloat16 [8, 4096, 8192], P('exp', None, ('ctx', 'dp')), may hold values from -0.09375 to 0.09375
- w_down: bfloat16 [8, 4096, 8192], P('exp', None, ('ctx', 'dp')), may hold values from -0.0625 to 0.0625
- out_grad: bfloat16 [2048, 4096], P('ctx', ('exp', 'dp')), may hold values from -6 to 6
Outputs:
- grad_residual: bfloat16 [2048, 4096], P('ctx', ('exp', 'dp'))
- grad_values: bfloat16 [2048, 4096], P('ctx', ('exp', 'dp'))
- grad_keys: float32 [2048, 64], P('ctx')
- grad_queries: float32 [2048, 64], P('ctx')
- grad_decay: float32 [2048, 64], P('ctx', ('exp', 'dp'))
- grad_probs: float32 [2048, 2], P('ctx')
- grad_gain: float32 [4096], P(('exp', 'dp'))
- w_gate_grad: bfloat16 [8, 4096, 8192], P('exp', None, ('ctx', 'dp'))
- w_up_grad: bfloat16 [8, 4096, 8192], P('exp', None, ('ctx', 'dp'))
- w_down_grad: bfloat16 [8, 4096, 8192], P('exp', None, ('ctx', 'dp'))
Inputs may be any that keep to these rules, and one draw needn't show every extreme that they name: `expert_ids`: each token names two different experts; among the 128 tokens of one index of ctx (aligned blocks) no expert is named more than 40 times, a bound that some block reaches. `log_decay`: negative everywhere.
All inputs are finite; a program needn't handle non-finite values.
Results may differ from a plain program's by a relative error of at most 0.028.
Values may be sent and summed in bfloat16 or wider, within the bound.
No kernel may reach another device: no remote copies, remote signals or barrier semaphores. Data moves between devices by JAX's collectives and lax.ppermute only.
A program may use at most 128 MiB of HBM per device.

v0:
```python
import jax
import jax.numpy as jnp
from jax import lax
from jax.sharding import PartitionSpec as P

HIGH = lax.Precision.HIGHEST
EPS = 1e-05


def entering(x, axis, join, neutral):
    place = lax.axis_index(axis)
    gathered = jax.tree.map(
        lambda a, kind: lax.all_gather(a.astype(kind), axis), x, (jnp.bfloat16, jnp.bfloat16)
    )
    state = jax.tree.map(lambda a, e: jnp.zeros_like(a) + jnp.asarray(e, a.dtype), x, neutral)

    def entering_one(step, state):
        return join(
            state,
            jax.tree.map(
                lambda a, own: lax.dynamic_index_in_dim(a, step, 0, False).astype(own.dtype),
                gathered,
                x,
            ),
        )

    return lax.fori_loop(0, place, entering_one, state)


def carried_in(x, axis, join, neutral):
    count = lax.axis_size(axis)
    place = lax.axis_index(axis)
    ahead = count - 1 - place
    gathered = jax.tree.map(
        lambda a, kind: lax.all_gather(a.astype(kind), axis),
        x,
        jax.tree.map(lambda a: jnp.bfloat16 if a.dtype == jnp.float32 else a.dtype, x),
    )
    state = jax.tree.map(lambda a, e: jnp.zeros_like(a) + jnp.asarray(e, a.dtype), x, neutral)

    def carried_one(step, state):
        source = count - 1 - step
        return join(
            state,
            jax.tree.map(
                lambda a, own: lax.dynamic_index_in_dim(a, source, 0, False).astype(own.dtype),
                gathered,
                x,
            ),
        )

    return lax.fori_loop(0, ahead, carried_one, state)


def block_state(values, key_rows, log_decay):
    cumulative = jnp.cumsum(log_decay, axis=0)
    total_log = cumulative[-1]
    tail_decay = jnp.exp(total_log[None, :] - cumulative)
    weighted = tail_decay[:, :, None] * values
    state_local = jnp.einsum("shp,sn->hpn", weighted, key_rows, precision=HIGH)
    return (jnp.exp(total_log), state_local)


def block_output(values, key_rows, queries, log_decay, state_in):
    cumulative = jnp.cumsum(log_decay, axis=0)
    length = values.shape[0]
    row_index = lax.broadcasted_iota(jnp.int32, (length, length), 0)
    col_index = lax.broadcasted_iota(jnp.int32, (length, length), 1)
    causal = (row_index >= col_index)[None]
    cum_heads = cumulative.T
    log_gap = jnp.where(causal, cum_heads[:, :, None] - cum_heads[:, None, :], 0.0)
    decay_mat = jnp.where(causal, jnp.exp(log_gap), 0.0)
    scores = jnp.dot(queries, key_rows.T, precision=HIGH)
    inner_part = jnp.einsum("hts,shp->thp", decay_mat * scores[None], values, precision=HIGH)
    carried = jnp.einsum("tn,hpn->thp", queries, state_in, precision=HIGH)
    return inner_part + jnp.exp(cumulative)[:, :, None] * carried


def silu_parts(gate_act):
    sigmoid_val = jax.nn.sigmoid(gate_act)
    return (gate_act * sigmoid_val, sigmoid_val * (1.0 + gate_act * (1.0 - sigmoid_val)))


def route_slots(token_ids, expert_count):
    owners = token_ids.reshape(-1)
    onehot = (owners[:, None] == jnp.arange(expert_count, dtype=jnp.int32)[None, :]).astype(
        jnp.int32
    )
    rank_before = jnp.cumsum(onehot, axis=0) - onehot
    return (owners, jnp.sum(rank_before * onehot, axis=1))


def combine_states(earlier_part, later_part):
    return (
        earlier_part[0] * later_part[0],
        later_part[0][:, None, None] * earlier_part[1] + later_part[1],
    )


def arrange_rows(gathered, ctx_count, dp_count):
    capacity = gathered.shape[1]
    exp_count = gathered.shape[2]
    feat = gathered.shape[3]
    shaped = gathered.reshape(ctx_count, dp_count, capacity, exp_count, feat)
    return shaped.transpose(0, 2, 3, 1, 4).reshape(
        ctx_count * capacity, exp_count * dp_count * feat
    )


def arrange_sums(full_term, ctx_count, dp_count, exp_count, capacity):
    feat = full_term.shape[1] // (exp_count * dp_count)
    shaped = full_term.reshape(ctx_count, capacity, exp_count, dp_count, feat)
    return shaped.transpose(0, 3, 1, 2, 4).reshape(
        ctx_count * dp_count * capacity, exp_count * feat
    )


def per_device(
    residual,
    ssm_values,
    ssm_keys,
    ssm_queries,
    log_decay,
    expert_ids,
    gate_probs,
    norm_gain,
    w_gate,
    w_up,
    w_down,
    out_grad,
):
    tokens = residual.shape[0]
    feat = residual.shape[1]
    heads_here = log_decay.shape[1]
    head_size = feat // heads_here
    model_width = w_gate.shape[1]
    ctx_count = lax.axis_size("ctx")
    exp_count = lax.axis_size("exp")
    dp_count = lax.axis_size("dp")
    expert_count = w_gate.shape[0] * exp_count
    capacity = 5 * tokens // (2 * expert_count)
    block_vals = ssm_values.astype(jnp.float32).reshape(tokens, heads_here, head_size)
    block_keys = ssm_keys.astype(jnp.float32)
    block_queries = ssm_queries.astype(jnp.float32)
    (decay_total, state_local), state_pull = jax.vjp(block_state, block_vals, block_keys, log_decay)
    neutral = (jnp.ones_like(decay_total), jnp.zeros_like(state_local))
    state_in = entering((decay_total, state_local), "ctx", combine_states, neutral)[1]
    mixer_out, output_pull = jax.vjp(
        block_output, block_vals, block_keys, block_queries, log_decay, state_in
    )
    hidden = (residual.astype(jnp.float32) + mixer_out.reshape(tokens, feat)).astype(jnp.bfloat16)
    hidden_f = hidden.astype(jnp.float32)
    square_sum = lax.psum(jnp.sum(hidden_f * hidden_f, axis=1), ("exp", "dp"))
    inv_rms = lax.rsqrt(square_sum / model_width + EPS)[:, None]
    normed = (hidden_f * inv_rms * norm_gain[None, :]).astype(jnp.bfloat16)
    owners, slot_index = route_slots(expert_ids, expert_count)
    pair_rows = jnp.repeat(normed, 2, axis=0)
    dout_rows = jnp.repeat(out_grad, 2, axis=0)
    pair_prob = gate_probs.reshape(-1)
    pair_cot = (pair_prob[:, None] * dout_rows.astype(jnp.float32)).astype(jnp.bfloat16)
    empty = jnp.zeros((expert_count, capacity, feat), jnp.bfloat16)
    send_rows = empty.at[owners, slot_index].set(pair_rows).reshape(expert_count, capacity, 1, feat)
    got_rows = lax.all_to_all(send_rows, "exp", split_axis=0, concat_axis=2, tiled=True)
    all_rows = lax.all_gather(got_rows, ("ctx", "dp"), axis=0, tiled=True)
    rows_flat = arrange_rows(all_rows, ctx_count, dp_count)
    act_gate = jnp.dot(rows_flat, w_gate[0], preferred_element_type=jnp.float32)
    act_up = jnp.dot(rows_flat, w_up[0], preferred_element_type=jnp.float32)
    swish_val, swish_slope = silu_parts(act_gate)
    hidden_act = (swish_val * act_up).astype(jnp.bfloat16)
    full_out = lax.dot_general(
        hidden_act, w_down[0], (((1,), (1,)), ((), ())), preferred_element_type=jnp.float32
    )
    out_total = lax.psum_scatter(
        arrange_sums(full_out, ctx_count, dp_count, exp_count, capacity).astype(jnp.bfloat16),
        ("ctx", "dp"),
        scatter_dimension=0,
        tiled=True,
    )
    expert_out = out_total.reshape(1, capacity, exp_count, feat)
    back_out = lax.all_to_all(expert_out, "exp", split_axis=2, concat_axis=0, tiled=True).reshape(
        expert_count, capacity, feat
    )
    out_pairs = back_out[owners, slot_index]
    probs_part = jnp.einsum(
        "kd,kd->k", out_pairs, dout_rows, preferred_element_type=jnp.float32
    ).reshape(tokens, 2)
    grad_probs = lax.psum(probs_part, ("exp", "dp"))
    send_cot = empty.at[owners, slot_index].set(pair_cot).reshape(expert_count, capacity, 1, feat)
    got_cot = lax.all_to_all(send_cot, "exp", split_axis=0, concat_axis=2, tiled=True)
    all_cot = lax.all_gather(got_cot, ("ctx", "dp"), axis=0, tiled=True)
    cot_flat = arrange_rows(all_cot, ctx_count, dp_count)
    grad_act = jnp.dot(cot_flat, w_down[0], preferred_element_type=jnp.float32)
    grad_gate = (grad_act * act_up * swish_slope).astype(jnp.bfloat16)
    grad_up = (grad_act * swish_val).astype(jnp.bfloat16)
    full_back = lax.dot_general(
        grad_gate, w_gate[0], (((1,), (1,)), ((), ())), preferred_element_type=jnp.float32
    ) + lax.dot_general(
        grad_up, w_up[0], (((1,), (1,)), ((), ())), preferred_element_type=jnp.float32
    )
    back_total = lax.psum_scatter(
        arrange_sums(full_back, ctx_count, dp_count, exp_count, capacity).astype(jnp.bfloat16),
        ("ctx", "dp"),
        scatter_dimension=0,
        tiled=True,
    )
    pair_back = back_total.reshape(1, capacity, exp_count, feat)
    back_in = lax.all_to_all(pair_back, "exp", split_axis=2, concat_axis=0, tiled=True).reshape(
        expert_count, capacity, feat
    )
    grad_normed = (
        back_in[owners, slot_index].astype(jnp.float32).reshape(tokens, 2, feat).sum(axis=1)
    )
    w_gate_grad = jnp.dot(rows_flat.T, grad_gate, preferred_element_type=jnp.float32).astype(
        jnp.bfloat16
    )[None]
    w_up_grad = jnp.dot(rows_flat.T, grad_up, preferred_element_type=jnp.float32).astype(
        jnp.bfloat16
    )[None]
    w_down_grad = jnp.dot(cot_flat.T, hidden_act, preferred_element_type=jnp.float32).astype(
        jnp.bfloat16
    )[None]
    scaled = grad_normed * norm_gain[None, :]
    inner_sum = lax.psum(jnp.sum(hidden_f * scaled, axis=1), ("exp", "dp"))
    projection = (inner_sum / model_width)[:, None]
    grad_hidden = (
        out_grad.astype(jnp.float32) + inv_rms * scaled - hidden_f * inv_rms**3 * projection
    )
    gain_part = jnp.sum(grad_normed * hidden_f * inv_rms, axis=0)
    grad_gain = lax.psum(gain_part, "ctx")
    grad_mixer = grad_hidden.reshape(tokens, heads_here, head_size)
    vals_first, keys_first, queries_part, decay_first, carry_cot = output_pull(grad_mixer)
    grad_state = carried_in((decay_total, carry_cot), "ctx", combine_states, neutral)[1]
    grad_total = jnp.sum(grad_state * state_in, axis=(1, 2))
    vals_second, keys_second, decay_second = state_pull((grad_total, grad_state))
    grad_keys, grad_queries = (
        lax.psum((keys_first + keys_second).astype(jnp.bfloat16), ("exp", "dp")).astype(
            jnp.float32
        ),
        lax.psum(queries_part.astype(jnp.bfloat16), ("exp", "dp")).astype(jnp.float32),
    )
    grad_residual = grad_hidden.astype(jnp.bfloat16)
    grad_values = (vals_first + vals_second).reshape(tokens, feat).astype(jnp.bfloat16)
    grad_decay = decay_first + decay_second
    return (
        grad_residual,
        grad_values,
        grad_keys,
        grad_queries,
        grad_decay,
        grad_probs,
        grad_gain,
        w_gate_grad,
        w_up_grad,
        w_down_grad,
    )


def solution(mesh):
    return jax.shard_map(
        per_device,
        mesh=mesh,
        in_specs=(
            P("ctx", ("exp", "dp")),
            P("ctx", ("exp", "dp")),
            P("ctx", None),
            P("ctx", None),
            P("ctx", ("exp", "dp")),
            P("ctx", None),
            P("ctx", None),
            P(("exp", "dp")),
            P("exp", None, ("ctx", "dp")),
            P("exp", None, ("ctx", "dp")),
            P("exp", None, ("ctx", "dp")),
            P("ctx", ("exp", "dp")),
        ),
        out_specs=(
            P("ctx", ("exp", "dp")),
            P("ctx", ("exp", "dp")),
            P("ctx", None),
            P("ctx", None),
            P("ctx", ("exp", "dp")),
            P("ctx", None),
            P(("exp", "dp")),
            P("exp", None, ("ctx", "dp")),
            P("exp", None, ("ctx", "dp")),
            P("exp", None, ("ctx", "dp")),
        ),
        check_vma=False,
    )
```

profile of v0, /device:TPU:2, one launch (start us, length us, event | category | flops | bytes accessed | tf_op | source)
XLA Modules:
  0.0 650.5 jit_solution(5369685150378966095)
XLA Ops:
  11.6 13.2 %scatter_fusion = bf16[8,40,256]{2,1,0:T(8,128)(2,1)S(1)} fusion(bf16[8,40,256]{2,1,0:T(8,128)(2,1)S(1)} %broadcast_in_dim.73.clone.1, s32[256]{0:T(256)S(1)} %bitcast.193, bf16[256,256]{1,0:T(8,128)(2,1)S(1)} %fusion.19), kind=kCustom, calls=%fused_computation.2 | custom fusion | bytes 395264 | tf_op jit(solution)/shard_map/scatter | solution.py:188
  24.9 18.0 %all_to_all.66 = bf16[8,40,1,256]{3,1,2,0:T(8,128)(2,1)S(1)} all-to-all(bf16[8,40,1,256]{3,1,2,0:T(8,128)(2,1)S(1)} %bitcast.200), channel_id=1, replica_groups=mesh['ctx'=16,'exp'=8,'dp'=2] {'exp'}, dimensions={0} | all-to-all | bytes 327680 | tf_op jit(solution)/shard_map/all_to_all | solution.py:189
  44.6 20.7 %all-gather.4 = bf16[16,1,4]{2,1,0:T(2,128)(2,1)S(1)} all-gather(bf16[1,1,4]{2,1,0:T(2,128)(2,1)S(1)} %get-tuple-element.299), channel_id=1, replica_groups=mesh['ctx'=16,'exp'=8,'dp'=2] {'ctx'}, dimensions={0}, use_global_device_ids=true | all-gather | bytes 136 | tf_op jit(solution)/shard_map/all_gather | solution.py:13
  67.0 27.6 %all-gather = bf16[64,64,64]{2,1,0:T(8,128)(2,1)} all-gather(bf16[4,64,64]{2,1,0:T(8,128)(2,1)S(1)} %convolution_convert_fusion.4), channel_id=2, replica_groups=mesh['ctx'=16,'exp'=8,'dp'=2] {'ctx'}, dimensions={0}, use_global_device_ids=true | all-gather | bytes 557056 | tf_op jit(solution)/shard_map/all_gather | solution.py:13
  96.7 23.5 %psum.42 = f32[128]{0:T(128)S(1)} all-reduce(f32[128]{0:T(128)S(1)} %get-tuple-element.291), channel_id=1, replica_groups=mesh['ctx'=16,'exp'=8,'dp'=2] {'exp','dp'}, use_global_device_ids=true, to_apply=%region_4.5 | all-reduce | flops 128 | bytes 1024 | tf_op jit(solution)/shard_map/psum | solution.py:153
  121.1 13.2 %scatter_fusion.1 = bf16[8,40,256]{2,1,0:T(8,128)(2,1)S(1)} fusion(bf16[8,40,256]{2,1,0:T(8,128)(2,1)S(1)} %broadcast_in_dim.73.clone, s32[256]{0:T(256)S(1)} %bitcast.194, bf16[256,256]{1,0:T(8,128)(2,1)S(1)} %reshape.273), kind=kCustom, calls=%fused_computation.3 | custom fusion | bytes 395264 | tf_op jit(solution)/shard_map/scatter | solution.py:162
  134.3 12.5 %all_to_all.67 = bf16[8,40,1,256]{3,1,2,0:T(8,128)(2,1)S(1)} all-to-all(bf16[8,40,1,256]{3,1,2,0:T(8,128)(2,1)S(1)} %bitcast.199), channel_id=1, replica_groups=mesh['ctx'=16,'exp'=8,'dp'=2] {'exp'}, dimensions={0} | all-to-all | bytes 327680 | tf_op jit(solution)/shard_map/all_to_all | solution.py:163
  148.1 13.0 %copy.164 = bf16[16,40,8,2,256]{4,3,2,1,0:T(2,128)(2,1)} copy(bf16[16,40,8,2,256]{4,2,1,3,0:T(8,128)(2,1)} %bitcast.203) | data formatting | bytes 10485760 | tf_op jit(solution)/shard_map/transpose | solution.py:105
  161.1 9.6 %reshape.236 = bf16[640,4096]{1,0:T(8,128)(2,1)} reshape(bf16[16,40,8,2,256]{4,3,2,1,0:T(2,128)(2,1)} %copy.164) | data formatting | bytes 10485760 | tf_op jit(solution)/shard_map/reshape | solution.py:105
  170.7 35.8 %all-gather.10.cloned.1.call-done = bf16[32,40,8,1,256]{4,2,3,1,0:T(8,128)(2,1)} async-done(((bf16[1,40,8,1,256]{4,2,3,1,0:T(8,128)(2,1)}), bf16[32,40,8,1,256]{4,2,3,1,0:T(8,128)(2,1)}) %all-gather.10.cloned.1.call-update) | async-done | bytes 5242896 | tf_op jit(solution)/shard_map/all_gather | solution.py:164
  206.6 13.0 %copy.167 = bf16[16,40,8,2,256]{4,3,2,1,0:T(2,128)(2,1)} copy(bf16[16,40,8,2,256]{4,2,1,3,0:T(8,128)(2,1)} %bitcast.204) | data formatting | bytes 10485760 | tf_op jit(solution)/shard_map/transpose | solution.py:105
  219.6 9.6 %reshape.240 = bf16[640,4096]{1,0:T(8,128)(2,1)} reshape(bf16[16,40,8,2,256]{4,3,2,1,0:T(2,128)(2,1)} %copy.167) | data formatting | bytes 10485760 | tf_op jit(solution)/shard_map/reshape | solution.py:105
  253.6 9.6 %convert_element_type.165 = bf16[16,40,8,2,256]{4,3,2,1,0:T(2,128)(2,1)} reshape(bf16[640,4096]{1,0:T(8,128)(2,1)} %add_convert_fusion) | data formatting | bytes 10485760 | tf_op jit(solution)/shard_map/convert_element_type | solution.py:201
  272.3 5.9 fusion.2
  278.2 60.3 %reduce-scatter.5.cloned.1.call-done = bf16[40,2048]{1,0:T(8,128)(2,1)} async-done(((bf16[1280,2048]{1,0:T(8,128)(2,1)}), bf16[40,2048]{1,0:T(8,128)(2,1)}) %reduce-scatter.5.cloned.1.call-update) | async-done | bytes 163856 | tf_op jit(solution)/shard_map/reduce_scatter | solution.py:173
  340.1 7.0 %all-to-all-start.3 = ((bf16[1,40,8,256]{3,1,0,2:T(8,128)(2,1)}), bf16[1,40,8,256]{3,1,0,2:T(8,128)(2,1)S(1)}, u32[]{:S(2)}, u32[]{:S(2)}) async-start(bf16[1,40,8,256]{3,1,0,2:T(8,128)(2,1)} %copy.177), calls=%async_computation.5 | async-start | bytes 327680 | tf_op jit(solution)/shard_map/all_to_all | solution.py:180
  347.2 5.7 fusion
  352.9 81.2 %reduce-scatter.3.cloned.1.call-done = bf16[40,2048]{1,0:T(8,128)(2,1)} async-done(((bf16[1280,2048]{1,0:T(8,128)(2,1)}), bf16[40,2048]{1,0:T(8,128)(2,1)}) %reduce-scatter.3.cloned.1.call-update) | async-done | bytes 163856 | tf_op jit(solution)/shard_map/reduce_scatter | solution.py:200
  435.8 7.2 %all-to-all-start.2 = ((bf16[1,40,8,256]{3,1,0,2:T(8,128)(2,1)}), bf16[1,40,8,256]{3,1,0,2:T(8,128)(2,1)S(1)}, u32[]{:S(2)}, u32[]{:S(2)}) async-start(bf16[1,40,8,256]{3,1,0,2:T(8,128)(2,1)} %copy.169), calls=%async_computation.3 | async-start | bytes 327680 | tf_op jit(solution)/shard_map/all_to_all | solution.py:207
  454.6 46.5 %all-reduce.1 = (f32[128]{0:T(128)S(1)}, f32[128,2]{1,0:T(8,128)S(1)}) all-reduce(f32[128]{0:T(128)S(1)} %get-tuple-element.264, f32[128,2]{1,0:T(8,128)S(1)} %reshape.247), channel_id=1, replica_groups=mesh['ctx'=16,'exp'=8,'dp'=2] {'exp','dp'}, use_global_device_ids=true, to_apply=%region_13.14 | all-reduce | flops 384 | bytes 3072 | tf_op jit(solution)/shard_map/psum | solution.py:223
  502.6 25.1 %all-gather.3 = bf16[64,64,64]{2,1,0:T(8,128)(2,1)} all-gather(bf16[4,64,64]{2,1,0:T(8,128)(2,1)S(1)} %convolution_convert_fusion.3), channel_id=5, replica_groups=mesh['ctx'=16,'exp'=8,'dp'=2] {'ctx'}, dimensions={0}, use_global_device_ids=true | all-gather | bytes 557056 | tf_op jit(solution)/shard_map/all_gather | solution.py:35
  527.7 22.9 %while.27 = (s32[]{:T(128)}, f32[4,64,64]{2,1,0:T(8,128)S(1)}, s32[]{:T(128)}, bf16[16,4]{1,0:T(8,128)(2,1)}, bf16[16,4,64,64]{3,2,1,0:T(8,128)(2,1)}, /*index=5*/s32[]{:T(128)}, s32[]{:T(128)}, s32[]{:T(128)}, s32[]{:T(128)}) while((s32[]{:T(128)}, f32[4,64,64]{2,1,0:T(8,128)S(1)}, s32[]{:T(128)}, bf16[16,4]{1,0:T(8,128)(2,1)}, ...), condition=%wide.region_15.16_spmd, body=%wide.region_14.15_spmd.sunk | while | flops 49162 | bytes 164035 | solution.py:52
  550.9 39.5 %psum.47 = f32[256]{0:T(256)} all-reduce(f32[256]{0:T(256)S(1)} %get-tuple-element.263), channel_id=1, replica_groups=mesh['ctx'=16,'exp'=8,'dp'=2] {'ctx'}, use_global_device_ids=true, to_apply=%region_30.31 | all-reduce | flops 256 | bytes 2048 | tf_op jit(solution)/shard_map/psum | solution.py:229
  593.7 45.7 %all-reduce.2 = (bf16[128,64]{0,1:T(8,128)(2,1)S(1)}, bf16[128,64]{0,1:T(8,128)(2,1)S(1)}) all-reduce(bf16[128,64]{0,1:T(8,128)(2,1)S(1)} %fusion.16, bf16[128,64]{0,1:T(8,128)(2,1)S(1)} %fusion.17), channel_id=1, replica_groups=mesh['ctx'=16,'exp'=8,'dp'=2] {'exp','dp'}, use_global_device_ids=true, to_apply=%region_17.18 | all-reduce | flops 16384 | bytes 65536 | tf_op jit(solution)/shard_map/psum | solution.py:236
  (179 shorter events, 93.0 us)
Async XLA Ops:
  7.2 222.0 %copy-start = (bf16[1,4096,256]{2,1,0:T(8,128)(2,1)S(1)}, bf16[1,4096,256]{2,1,0:T(8,128)(2,1)}, u32[]{:S(2)}) copy-start(bf16[1,4096,256]{2,1,0:T(8,128)(2,1)} %param.26) | copy-start | bytes 6291460
  7.2 59.6 %copy-start.13 = (bf16[128,64]{0,1:T(8,128)(2,1)S(1)}, bf16[128,64]{0,1:T(8,128)(2,1)}, u32[]{:S(2)}) copy-start(bf16[128,64]{0,1:T(8,128)(2,1)} %param.18) | copy-start | bytes 49156
  7.2 87.4 %copy-start.12 = (bf16[128,64]{0,1:T(8,128)(2,1)S(1)}, bf16[128,64]{0,1:T(8,128)(2,1)}, u32[]{:S(2)}) copy-start(bf16[128,64]{0,1:T(8,128)(2,1)} %param.19) | copy-start | bytes 49156
  7.2 89.4 %copy-start.16 = (bf16[128,256]{1,0:T(8,128)(2,1)S(1)}, bf16[128,256]{1,0:T(8,128)(2,1)}, u32[]{:S(2)}) copy-start(bf16[128,256]{1,0:T(8,128)(2,1)} %param.16) | copy-start | bytes 196612
  7.2 113.6 %copy-start.17 = (f32[256]{0:T(256)S(1)}, f32[256]{0:T(256)}, u32[]{:S(2)}) copy-start(f32[256]{0:T(256)} %param.23) | copy-start | bytes 3076
  7.2 140.9 %all-gather.8.cloned.1.call-start = ((), (), s32[]{:S(2)}) async-start(), calls=%async_computation.8 | async-start | bytes 5406720 | tf_op jit(solution)/shard_map/all_gather | solution.py:190
  43.6 163.0 %all-gather.10.cloned.1.call-start = ((), (), s32[]{:S(2)}) async-start(), calls=%async_computation.9 | async-start | bytes 5406720 | tf_op jit(solution)/shard_map/all_gather | solution.py:164
  66.4 67.9 %copy-start.19 = (f32[4,128]{1,0:T(4,128)}, f32[4,128]{1,0:T(4,128)S(1)}, u32[]{:S(2)}) copy-start(f32[4,128]{1,0:T(4,128)S(1)} %copy.150) | copy-start | bytes 6148
  94.8 39.5 %copy-start.14 = (f32[128,128]{1,0:T(8,128)}, f32[128,128]{1,0:T(8,128)S(1)}, u32[]{:S(2)}) copy-start(f32[128,128]{1,0:T(8,128)S(1)} %fusion.65) | copy-start | bytes 196612
  95.8 38.5 %copy-start.18 = (bf16[16,4]{1,0:T(8,128)(2,1)}, bf16[16,4]{1,0:T(8,128)(2,1)S(1)}, u32[]{:S(2)}) copy-start(bf16[16,4]{1,0:T(8,128)(2,1)S(1)} %get-tuple-element.437) | copy-start | bytes 388
  147.5 191.0 %reduce-scatter.5.cloned.1.call-start = ((), (), s32[]{:S(2)}) async-start(), calls=%async_computation.7 | async-start | bytes 5406720 | tf_op jit(solution)/shard_map/reduce_scatter | solution.py:173
  229.2 4.2 copy-start.2
  229.2 4.7 copy-start.3
  238.0 3.9 copy-start.9
  246.6 187.5 %reduce-scatter.3.cloned.1.call-start = ((), (), s32[]{:S(2)}) async-start(), calls=%async_computation.6 | async-start | bytes 5406720 | tf_op jit(solution)/shard_map/reduce_scatter | solution.py:200
  248.2 1.6 copy-start.7
  340.1 95.7 %all-to-all-start.3 = ((bf16[1,40,8,256]{3,1,0,2:T(8,128)(2,1)}), bf16[1,40,8,256]{3,1,0,2:T(8,128)(2,1)S(1)}, u32[]{:S(2)}, u32[]{:S(2)}) async-start(bf16[1,40,8,256]{3,1,0,2:T(8,128)(2,1)} %copy.177), calls=%async_computation.5 | async-start | bytes 327680 | tf_op jit(solution)/shard_map/all_to_all | solution.py:180
  347.2 95.8 %copy-start.8 = (bf16[640,256]{1,0:T(8,128)(2,1)S(1)}, bf16[640,256]{1,0:T(8,128)(2,1)}, u32[]{:S(2)}) copy-start(bf16[640,256]{1,0:T(8,128)(2,1)} %get-tuple-element.297) | copy-start | bytes 983044
  435.8 16.6 %all-to-all-start.2 = ((bf16[1,40,8,256]{3,1,0,2:T(8,128)(2,1)}), bf16[1,40,8,256]{3,1,0,2:T(8,128)(2,1)S(1)}, u32[]{:S(2)}, u32[]{:S(2)}) async-start(bf16[1,40,8,256]{3,1,0,2:T(8,128)(2,1)} %copy.169), calls=%async_computation.3 | async-start | bytes 327680 | tf_op jit(solution)/shard_map/all_to_all | solution.py:207
  443.0 58.1 %copy-start.11 = (bf16[128,256]{1,0:T(8,128)(2,1)S(1)}, bf16[128,256]{1,0:T(8,128)(2,1)}, u32[]{:S(2)}) copy-start(bf16[128,256]{1,0:T(8,128)(2,1)} %param.27) | copy-start | bytes 196612
  443.0 58.1 %copy-start.21 = (f32[128]{0:T(128)S(1)}, f32[128]{0:T(128)}, u32[]{:S(2)}) copy-start(f32[128]{0:T(128)} %get-tuple-element.300) | copy-start | bytes 1540
  448.7 142.3 %copy-start.15 = (f32[128,128]{1,0:T(8,128)S(1)}, f32[128,128]{1,0:T(8,128)}, u32[]{:S(2)}) copy-start(f32[128,128]{1,0:T(8,128)} %copy-done.14) | copy-start | bytes 196612
  448.7 142.3 %copy-start.20 = (f32[4,128]{1,0:T(4,128)S(1)}, f32[4,128]{1,0:T(4,128)}, u32[]{:S(2)}) copy-start(f32[4,128]{1,0:T(4,128)} %copy-done.19) | copy-start | bytes 6148
  452.4 191.4 %copy-start.1 = (bf16[1,4096,256]{2,1,0:T(8,128)(2,1)S(1)}, bf16[1,4096,256]{2,1,0:T(8,128)(2,1)}, u32[]{:S(2)}) copy-start(bf16[1,4096,256]{2,1,0:T(8,128)(2,1)} %param.26) | copy-start | bytes 6291460
  (4 other events, 5.8 us)
Sparse Core Ops, SparseCore 0:
  43.7 49.1 all-gather.7
  147.6 58.8 all-gather.9
  246.7 91.7 reduce-scatter.4
  342.4 91.7 reduce-scatter.2
where the time goes:
time: 657 us; the launch traced here: 650 us
  blocking collectives  259 us (39%)
  waiting for transfers between devices  179 us (27%)
  local copies, waits for them, and re-layouts  116 us (18%)
  matrix products  35.9 us (5%)
  other arithmetic  30.4 us (5%)
  starting transfers between devices  15.3 us (2%)
  between operations  14.5 us (2%)
    reduce_scatter x1, waiting for transfers between devices, per_device(): lax.psum_scatter(arrange_sums(full_back, ctx_count, dp_count, exp_count,...  81.2 us
    reduce_scatter x1, waiting for transfers between devices, per_device(): lax.psum_scatter(arrange_sums(full_out, ctx_count, dp_count, exp_count, c...  60.3 us
    all_gather x2, blocking collectives, entering(): lax.all_gather(a.astype(kind), axis)  48.3 us
    psum x1, blocking collectives, per_device(): inner_sum = lax.psum(jnp.sum(hidden_f * scaled, axis=1), ('exp', 'dp'))  46.5 us
    psum x1, blocking collectives, per_device(): lax.psum((keys_first + keys_second).astype(jnp.bfloat16), ('exp', 'dp'))  45.7 us
    psum x1, blocking collectives, per_device(): grad_gain = lax.psum(gain_part, 'ctx')  39.5 us
    all_gather x1, waiting for transfers between devices, per_device(): all_rows = lax.all_gather(got_rows, ('ctx', 'dp'), axis=0, tiled=True)  35.8 us
    transpose x2, local copies, waits for them, and re-layouts, arrange_rows(): shaped.transpose(0, 2, 3, 1, 4)  26 us
  transfers between devices with their start and end apart: 6, of which 4 were waited for; matrix products, arithmetic and copies ran while one was open for 13% of the time, Pallas kernels for 0%

commit v1 on v0

--- a/solution.py
+++ b/solution.py
@@ -1,3 +1,4 @@
+import functools
 import jax
 import jax.numpy as jnp
 from jax import lax
@@ -5,6 +6,22 @@
 
 HIGH = lax.Precision.HIGHEST
 EPS = 1e-05
+
+
+def advance_circles_on(xin, axis_tag, pos_dim):
+    part_now = jnp.concatenate(
+        lax.all_to_all(
+            jnp.stack(lax.axis_size(axis_tag) * [xin]),
+            split_axis=0,
+            concat_axis=0,
+            axis_name=axis_tag,
+        ),
+        pos_dim,
+    )
+    return part_now
+
+
+keys_form = functools.partial(advance_circles_on, axis_tag=("ctx", "dp"), pos_dim=0)
 
 
 def entering(x, axis, join, neutral):
@@ -161,7 +178,7 @@
     empty = jnp.zeros((expert_count, capacity, feat), jnp.bfloat16)
     send_rows = empty.at[owners, slot_index].set(pair_rows).reshape(expert_count, capacity, 1, feat)
     got_rows = lax.all_to_all(send_rows, "exp", split_axis=0, concat_axis=2, tiled=True)
-    all_rows = lax.all_gather(got_rows, ("ctx", "dp"), axis=0, tiled=True)
+    all_rows = keys_form(got_rows)
     rows_flat = arrange_rows(all_rows, ctx_count, dp_count)
     act_gate = jnp.dot(rows_flat, w_gate[0], preferred_element_type=jnp.float32)
     act_up = jnp.dot(rows_flat, w_up[0], preferred_element_type=jnp.float32)

time: 657 us -> 701 us (1.067)
  blocking collectives: 259 us -> 338 us
  waiting for transfers between devices: 179 us -> 137 us
    all_to_all x0 -> x1, blocking collectives: none -> 79.4 us  [advance_circles_on(): lax.all_to_all(jnp.stack(lax.axis_size(axis_tag) * [xin]), split_axis=0,...]
    all_gather x1 -> x0, waiting for transfers between devices: 35.8 us -> none  [per_device(): all_rows = lax.all_gather(got_rows, ('ctx', 'dp'), axis=0, tiled=True)]
    unnamed x55 -> x53, local copies, waits for them, and re-layouts: 19.4 us -> 19 us
  transfers between devices with their start and end apart: 6 -> 5, of which waited for: 4 -> 3; matrix products, arithmetic and copies ran while one was open for 13% -> 13% of each run, Pallas kernels for 0% -> 0%
where the time goes in v1:
time: 701 us; the launch traced here: 694 us
  blocking collectives  338 us (48%)
  waiting for transfers between devices  137 us (20%)
  local copies, waits for them, and re-layouts  116 us (17%)
  matrix products  42.4 us (6%)
  other arithmetic  30.4 us (4%)
  starting transfers between devices  14.6 us (2%)
  between operations  14.5 us (2%)
    reduce_scatter x1, waiting for transfers between devices, per_device(): lax.psum_scatter(arrange_sums(full_back, ctx_count, dp_count, exp_count,...  81.4 us
    all_to_all x1, blocking collectives, advance_circles_on(): lax.all_to_all(jnp.stack(lax.axis_size(axis_tag) * [xin]), split_axis=0,...  79.4 us
    reduce_scatter x1, waiting for transfers between devices, per_device(): lax.psum_scatter(arrange_sums(full_out, ctx_count, dp_count, exp_count, c...  54.2 us
    all_gather x2, blocking collectives, entering(): lax.all_gather(a.astype(kind), axis)  48.3 us
    psum x1, blocking collectives, per_device(): inner_sum = lax.psum(jnp.sum(hidden_f * scaled, axis=1), ('exp', 'dp'))  46.5 us
    psum x1, blocking collectives, per_device(): lax.psum((keys_first + keys_second).astype(jnp.bfloat16), ('exp', 'dp'))  45.7 us
    psum x1, blocking collectives, per_device(): grad_gain = lax.psum(gain_part, 'ctx')  39.5 us
    transpose x2, local copies, waits for them, and re-layouts, arrange_rows(): shaped.transpose(0, 2, 3, 1, 4)  26 us
  transfers between devices with their start and end apart: 5, of which 3 were waited for; matrix products, arithmetic and copies ran while one was open for 13% of the time, Pallas kernels for 0%

profile of v1, /device:TPU:2, one launch (start us, length us, event | category | flops | bytes accessed | tf_op | source)
XLA Modules:
  0.0 693.6 jit_solution(12553914316293552880)
XLA Ops:
  11.6 13.2 %scatter_fusion = bf16[8,40,256]{2,1,0:T(8,128)(2,1)S(1)} fusion(bf16[8,40,256]{2,1,0:T(8,128)(2,1)S(1)} %broadcast_in_dim.73.clone.1, s32[256]{0:T(256)S(1)} %bitcast.195, bf16[256,256]{1,0:T(8,128)(2,1)S(1)} %fusion.19), kind=kCustom, calls=%fused_computation.2 | custom fusion | bytes 395264 | tf_op jit(solution)/shard_map/scatter | solution.py:205
  24.9 18.0 %all_to_all.68 = bf16[8,40,1,256]{3,1,2,0:T(8,128)(2,1)S(1)} all-to-all(bf16[8,40,1,256]{3,1,2,0:T(8,128)(2,1)S(1)} %bitcast.203), channel_id=1, replica_groups=mesh['ctx'=16,'exp'=8,'dp'=2] {'exp'}, dimensions={0} | all-to-all | bytes 327680 | tf_op jit(solution)/shard_map/all_to_all | solution.py:206
  44.6 20.7 %all-gather.3 = bf16[16,1,4]{2,1,0:T(2,128)(2,1)S(1)} all-gather(bf16[1,1,4]{2,1,0:T(2,128)(2,1)S(1)} %get-tuple-element.299), channel_id=1, replica_groups=mesh['ctx'=16,'exp'=8,'dp'=2] {'ctx'}, dimensions={0}, use_global_device_ids=true | all-gather | bytes 136 | tf_op jit(solution)/shard_map/all_gather | solution.py:30
  67.0 27.6 %all-gather = bf16[64,64,64]{2,1,0:T(8,128)(2,1)} all-gather(bf16[4,64,64]{2,1,0:T(8,128)(2,1)S(1)} %convolution_convert_fusion.4), channel_id=2, replica_groups=mesh['ctx'=16,'exp'=8,'dp'=2] {'ctx'}, dimensions={0}, use_global_device_ids=true | all-gather | bytes 557056 | tf_op jit(solution)/shard_map/all_gather | solution.py:30
  96.7 23.5 %psum.42 = f32[128]{0:T(128)S(1)} all-reduce(f32[128]{0:T(128)S(1)} %get-tuple-element.291), channel_id=1, replica_groups=mesh['ctx'=16,'exp'=8,'dp'=2] {'exp','dp'}, use_global_device_ids=true, to_apply=%region_4.5 | all-reduce | flops 128 | bytes 1024 | tf_op jit(solution)/shard_map/psum | solution.py:170
  121.1 13.2 %scatter_fusion.1 = bf16[8,40,256]{2,1,0:T(8,128)(2,1)S(1)} fusion(bf16[8,40,256]{2,1,0:T(8,128)(2,1)S(1)} %broadcast_in_dim.73.clone, s32[256]{0:T(256)S(1)} %bitcast.196, bf16[256,256]{1,0:T(8,128)(2,1)S(1)} %reshape.274), kind=kCustom, calls=%fused_computation.3 | custom fusion | bytes 395264 | tf_op jit(solution)/shard_map/scatter | solution.py:179
  134.3 12.5 %all_to_all.69 = bf16[8,40,1,256]{3,1,2,0:T(8,128)(2,1)S(1)} all-to-all(bf16[8,40,1,256]{3,1,2,0:T(8,128)(2,1)S(1)} %bitcast.202), channel_id=1, replica_groups=mesh['ctx'=16,'exp'=8,'dp'=2] {'exp'}, dimensions={0} | all-to-all | bytes 327680 | tf_op jit(solution)/shard_map/all_to_all | solution.py:180
  147.4 79.4 %all_to_all.70 = bf16[32,1,40,8,256]{4,3,2,1,0:T(8,128)(2,1)} all-to-all(bf16[32,1,40,8,256]{4,3,2,1,0:T(8,128)(2,1)S(1)} %stack.5), channel_id=1, replica_groups=mesh['ctx'=16,'exp'=8,'dp'=2] {'ctx','dp'}, dimensions={0} | all-to-all | bytes 10485760 | tf_op jit(solution)/shard_map/all_to_all | solution.py:13
  226.8 13.0 %copy.169 = bf16[16,40,8,2,256]{4,3,2,1,0:T(2,128)(2,1)} copy(bf16[16,40,8,2,256]{4,2,1,3,0:T(8,128)(2,1)} %bitcast.199) | data formatting | bytes 10485760 | tf_op jit(solution)/shard_map/transpose | solution.py:122
  239.8 9.6 %reshape.241 = bf16[640,4096]{1,0:T(8,128)(2,1)} reshape(bf16[16,40,8,2,256]{4,3,2,1,0:T(2,128)(2,1)} %copy.169) | data formatting | bytes 10485760 | tf_op jit(solution)/shard_map/reshape | solution.py:122
  255.0 13.0 %copy.166 = bf16[16,40,8,2,256]{4,3,2,1,0:T(2,128)(2,1)} copy(bf16[16,40,8,2,256]{4,2,1,3,0:T(8,128)(2,1)} %bitcast.206) | data formatting | bytes 10485760 | tf_op jit(solution)/shard_map/transpose | solution.py:122
  268.0 9.8 %reshape.238 = bf16[640,4096]{1,0:T(8,128)(2,1)} reshape(bf16[16,40,8,2,256]{4,3,2,1,0:T(2,128)(2,1)} %copy.166) | data formatting | bytes 10485760 | tf_op jit(solution)/shard_map/reshape | solution.py:122
  302.6 9.7 %convert_element_type.165 = bf16[16,40,8,2,256]{4,3,2,1,0:T(2,128)(2,1)} reshape(bf16[640,4096]{1,0:T(8,128)(2,1)} %add_convert_fusion) | data formatting | bytes 10485760 | tf_op jit(solution)/shard_map/convert_element_type | solution.py:218
  321.4 5.9 fusion.2
  327.2 54.2 %reduce-scatter.5.cloned.1.call-done = bf16[40,2048]{1,0:T(8,128)(2,1)} async-done(((bf16[1280,2048]{1,0:T(8,128)(2,1)}), bf16[40,2048]{1,0:T(8,128)(2,1)}) %reduce-scatter.5.cloned.1.call-update) | async-done | bytes 163856 | tf_op jit(solution)/shard_map/reduce_scatter | solution.py:190
  383.1 7.0 %all-to-all-start.4 = ((bf16[1,40,8,256]{3,1,0,2:T(8,128)(2,1)}), bf16[1,40,8,256]{3,1,0,2:T(8,128)(2,1)S(1)}, u32[]{:S(2)}, u32[]{:S(2)}) async-start(bf16[1,40,8,256]{3,1,0,2:T(8,128)(2,1)} %copy.179), calls=%async_computation.6 | async-start | bytes 327680 | tf_op jit(solution)/shard_map/all_to_all | solution.py:197
  390.1 5.7 fusion
  395.8 81.4 %reduce-scatter.3.cloned.1.call-done = bf16[40,2048]{1,0:T(8,128)(2,1)} async-done(((bf16[1280,2048]{1,0:T(8,128)(2,1)}), bf16[40,2048]{1,0:T(8,128)(2,1)}) %reduce-scatter.3.cloned.1.call-update) | async-done | bytes 163856 | tf_op jit(solution)/shard_map/reduce_scatter | solution.py:217
  478.8 7.3 %all-to-all-start.3 = ((bf16[1,40,8,256]{3,1,0,2:T(8,128)(2,1)}), bf16[1,40,8,256]{3,1,0,2:T(8,128)(2,1)S(1)}, u32[]{:S(2)}, u32[]{:S(2)}) async-start(bf16[1,40,8,256]{3,1,0,2:T(8,128)(2,1)} %copy.171), calls=%async_computation.4 | async-start | bytes 327680 | tf_op jit(solution)/shard_map/all_to_all | solution.py:224
  497.8 46.5 %all-reduce.1 = (f32[128]{0:T(128)S(1)}, f32[128,2]{1,0:T(8,128)S(1)}) all-reduce(f32[128]{0:T(128)S(1)} %get-tuple-element.264, f32[128,2]{1,0:T(8,128)S(1)} %reshape.248), channel_id=1, replica_groups=mesh['ctx'=16,'exp'=8,'dp'=2] {'exp','dp'}, use_global_device_ids=true, to_apply=%region_13.14 | all-reduce | flops 384 | bytes 3072 | tf_op jit(solution)/shard_map/psum | solution.py:240
  545.7 25.0 %all-gather.2 = bf16[64,64,64]{2,1,0:T(8,128)(2,1)} all-gather(bf16[4,64,64]{2,1,0:T(8,128)(2,1)S(1)} %convolution_convert_fusion.3), channel_id=4, replica_groups=mesh['ctx'=16,'exp'=8,'dp'=2] {'ctx'}, dimensions={0}, use_global_device_ids=true | all-gather | bytes 557056 | tf_op jit(solution)/shard_map/all_gather | solution.py:52
  570.8 22.9 %while.27 = (s32[]{:T(128)}, f32[4,64,64]{2,1,0:T(8,128)S(1)}, s32[]{:T(128)}, bf16[16,4]{1,0:T(8,128)(2,1)}, bf16[16,4,64,64]{3,2,1,0:T(8,128)(2,1)}, /*index=5*/s32[]{:T(128)}, s32[]{:T(128)}, s32[]{:T(128)}, s32[]{:T(128)}) while((s32[]{:T(128)}, f32[4,64,64]{2,1,0:T(8,128)S(1)}, s32[]{:T(128)}, bf16[16,4]{1,0:T(8,128)(2,1)}, ...), condition=%wide.region_15.16_spmd, body=%wide.region_14.15_spmd.sunk | while | flops 49162 | bytes 164035 | solution.py:69
  594.0 39.5 %psum.47 = f32[256]{0:T(256)} all-reduce(f32[256]{0:T(256)S(1)} %get-tuple-element.263), channel_id=1, replica_groups=mesh['ctx'=16,'exp'=8,'dp'=2] {'ctx'}, use_global_device_ids=true, to_apply=%region_30.31 | all-reduce | flops 256 | bytes 2048 | tf_op jit(solution)/shard_map/psum | solution.py:246
  636.8 45.7 %all-reduce.2 = (bf16[128,64]{0,1:T(8,128)(2,1)S(1)}, bf16[128,64]{0,1:T(8,128)(2,1)S(1)}) all-reduce(bf16[128,64]{0,1:T(8,128)(2,1)S(1)} %fusion.16, bf16[128,64]{0,1:T(8,128)(2,1)S(1)} %fusion.17), channel_id=1, replica_groups=mesh['ctx'=16,'exp'=8,'dp'=2] {'exp','dp'}, use_global_device_ids=true, to_apply=%region_17.18 | all-reduce | flops 16384 | bytes 65536 | tf_op jit(solution)/shard_map/psum | solution.py:253
  (176 shorter events, 98.2 us)
Async XLA Ops:
  7.2 270.6 %copy-start = (bf16[1,4096,256]{2,1,0:T(8,128)(2,1)S(1)}, bf16[1,4096,256]{2,1,0:T(8,128)(2,1)}, u32[]{:S(2)}) copy-start(bf16[1,4096,256]{2,1,0:T(8,128)(2,1)} %param.26) | copy-start | bytes 6291460
  7.2 59.6 %copy-start.11 = (bf16[128,64]{0,1:T(8,128)(2,1)S(1)}, bf16[128,64]{0,1:T(8,128)(2,1)}, u32[]{:S(2)}) copy-start(bf16[128,64]{0,1:T(8,128)(2,1)} %param.18) | copy-start | bytes 49156
  7.2 87.4 %copy-start.10 = (bf16[128,64]{0,1:T(8,128)(2,1)S(1)}, bf16[128,64]{0,1:T(8,128)(2,1)}, u32[]{:S(2)}) copy-start(bf16[128,64]{0,1:T(8,128)(2,1)} %param.19) | copy-start | bytes 49156
  7.2 89.4 %copy-start.14 = (bf16[128,256]{1,0:T(8,128)(2,1)S(1)}, bf16[128,256]{1,0:T(8,128)(2,1)}, u32[]{:S(2)}) copy-start(bf16[128,256]{1,0:T(8,128)(2,1)} %param.16) | copy-start | bytes 196612
  7.2 113.6 %copy-start.15 = (f32[256]{0:T(256)S(1)}, f32[256]{0:T(256)}, u32[]{:S(2)}) copy-start(f32[256]{0:T(256)} %param.23) | copy-start | bytes 3076
  7.2 247.8 %all-gather.6.cloned.1.call-start = ((), (), s32[]{:S(2)}) async-start(), calls=%async_computation.9 | async-start | bytes 5406720 | tf_op jit(solution)/shard_map/all_gather | solution.py:207
  43.6 337.8 %reduce-scatter.5.cloned.1.call-start = ((), (), s32[]{:S(2)}) async-start(), calls=%async_computation.8 | async-start | bytes 5406720 | tf_op jit(solution)/shard_map/reduce_scatter | solution.py:190
  66.4 67.9 %copy-start.17 = (f32[4,128]{1,0:T(4,128)}, f32[4,128]{1,0:T(4,128)S(1)}, u32[]{:S(2)}) copy-start(f32[4,128]{1,0:T(4,128)S(1)} %copy.152) | copy-start | bytes 6148
  94.8 39.5 %copy-start.12 = (f32[128,128]{1,0:T(8,128)}, f32[128,128]{1,0:T(8,128)S(1)}, u32[]{:S(2)}) copy-start(f32[128,128]{1,0:T(8,128)S(1)} %fusion.65) | copy-start | bytes 196612
  95.8 38.5 %copy-start.16 = (bf16[16,4]{1,0:T(8,128)(2,1)}, bf16[16,4]{1,0:T(8,128)(2,1)S(1)}, u32[]{:S(2)}) copy-start(bf16[16,4]{1,0:T(8,128)(2,1)S(1)} %get-tuple-element.433) | copy-start | bytes 388
  277.8 4.2 copy-start.3
  277.8 4.2 copy-start.20
  287.0 3.9 copy-start.7
  295.6 1.6 copy-start.2
  295.6 181.6 %reduce-scatter.3.cloned.1.call-start = ((), (), s32[]{:S(2)}) async-start(), calls=%async_computation.7 | async-start | bytes 5406720 | tf_op jit(solution)/shard_map/reduce_scatter | solution.py:217
  297.2 1.6 copy-start.5
  383.1 95.8 %all-to-all-start.4 = ((bf16[1,40,8,256]{3,1,0,2:T(8,128)(2,1)}), bf16[1,40,8,256]{3,1,0,2:T(8,128)(2,1)S(1)}, u32[]{:S(2)}, u32[]{:S(2)}) async-start(bf16[1,40,8,256]{3,1,0,2:T(8,128)(2,1)} %copy.179), calls=%async_computation.6 | async-start | bytes 327680 | tf_op jit(solution)/shard_map/all_to_all | solution.py:197
  390.1 96.0 %copy-start.6 = (bf16[640,256]{1,0:T(8,128)(2,1)S(1)}, bf16[640,256]{1,0:T(8,128)(2,1)}, u32[]{:S(2)}) copy-start(bf16[640,256]{1,0:T(8,128)(2,1)} %get-tuple-element.297) | copy-start | bytes 983044
  478.8 16.7 %all-to-all-start.3 = ((bf16[1,40,8,256]{3,1,0,2:T(8,128)(2,1)}), bf16[1,40,8,256]{3,1,0,2:T(8,128)(2,1)S(1)}, u32[]{:S(2)}, u32[]{:S(2)}) async-start(bf16[1,40,8,256]{3,1,0,2:T(8,128)(2,1)} %copy.171), calls=%async_computation.4 | async-start | bytes 327680 | tf_op jit(solution)/shard_map/all_to_all | solution.py:224
  486.1 58.1 %copy-start.9 = (bf16[128,256]{1,0:T(8,128)(2,1)S(1)}, bf16[128,256]{1,0:T(8,128)(2,1)}, u32[]{:S(2)}) copy-start(bf16[128,256]{1,0:T(8,128)(2,1)} %param.27) | copy-start | bytes 196612
  486.1 58.1 %copy-start.19 = (f32[128]{0:T(128)S(1)}, f32[128]{0:T(128)}, u32[]{:S(2)}) copy-start(f32[128]{0:T(128)} %get-tuple-element.300) | copy-start | bytes 1540
  491.8 142.3 %copy-start.13 = (f32[128,128]{1,0:T(8,128)S(1)}, f32[128,128]{1,0:T(8,128)}, u32[]{:S(2)}) copy-start(f32[128,128]{1,0:T(8,128)} %copy-done.12) | copy-start | bytes 196612
  491.8 142.3 %copy-start.18 = (f32[4,128]{1,0:T(4,128)S(1)}, f32[4,128]{1,0:T(4,128)}, u32[]{:S(2)}) copy-start(f32[4,128]{1,0:T(4,128)} %copy-done.17) | copy-start | bytes 6148
  495.5 191.3 %copy-start.1 = (bf16[1,4096,256]{2,1,0:T(8,128)(2,1)S(1)}, bf16[1,4096,256]{2,1,0:T(8,128)(2,1)}, u32[]{:S(2)}) copy-start(bf16[1,4096,256]{2,1,0:T(8,128)(2,1)} %param.26) | copy-start | bytes 6291460
  (2 other events, 2.6 us)
Sparse Core Ops, SparseCore 0:
  43.7 49.1 all-gather.5
  295.7 85.6 reduce-scatter.4
  385.4 91.7 reduce-scatter.2
